TPU v7x, 256 devices: a whole 4x4x8 slice. The times are simulated.
256 devices in a mesh: tp: 8 (over x, core), ad: 32 (over y, z).
Axes of the slice: x: 4, y: 4, z: 8, core: 2. Of those that a mesh axis runs over, the one named last changes fastest.
Arguments:
- hidden: bfloat16 [14336, 8192], P('ad'), may hold values from -6 to 6
- gain: bfloat16 [8192], replicated, may hold values from 0.25 to 1.75
- key_value_weight: bfloat16 [8192, 2, 1024], P(None, None, 'tp'), may hold values from -0.0625 to 0.0625
- adapter_down_weight: bfloat16 [64, 8192, 128], P('ad', 'tp'), may hold values from -0.0625 to 0.0625
- adapter_up_weight: bfloat16 [64, 2, 64, 1024], P('ad', None, None, 'tp'), may hold values from -0.75 to 0.75
- language_pair_index: int32 [14336], P('ad'), may hold values from 0 to 63, as said below
- adapter_row_index: int32 [64], replicated, may hold values from 0 to 63, as said below
Outputs:
- kv_out: bfloat16 [14336, 2, 1024], P('ad', None, 'tp')
Inputs may be any that keep to these rules, and one draw needn't show every extreme that they name: A row's owner is adapter_row_index[language_pair_index] // 2. Among the rows of one device, one owner, the same for every device, has exactly 56 rows; every other owner has at most 28, and one other owner, the same for every device, exactly 28. `adapter_row_index`: each adapter's row in adapter_down_weight and adapter_up_weight; every row appears once.
All inputs are finite; a program needn't handle non-finite values.
Results may differ from a plain program's by a relative error of at most 0.0053.
Values may be sent and summed in bfloat16 or wider, within the bound.
No kernel may reach another device: no remote copies, remote signals or barrier semaphores. Data moves between devices by JAX's collectives and lax.ppermute only.
A program may use at most 128 MiB of HBM per device.

v0:
```python
import jax
import jax.numpy as jnp
from jax import lax
from jax.sharding import PartitionSpec as P

epsilon = 1e-05
adapter_scale = 0.5


def down_local(rows_in, row_ids, down_table):
    adapter_total = down_table.shape[0]
    labels = jnp.arange(adapter_total, dtype=jnp.int32)
    row_mask = row_ids[:, None] == labels[None, :]
    every_low = jnp.einsum("rc,acm->ram", rows_in, down_table, preferred_element_type=jnp.float32)
    partial_low = jnp.sum(jnp.where(row_mask[:, :, None], every_low, jnp.float32(0.0)), axis=1)
    return (partial_low, row_mask)


def upward_delta(summed_low, row_mask, up_table):
    narrow = summed_low.astype(jnp.bfloat16)
    row_total = narrow.shape[0]
    adapter_total = up_table.shape[0]
    rank_width = up_table.shape[2]
    widened = jnp.where(row_mask[:, :, None], narrow[:, None, :], jnp.zeros((), jnp.bfloat16))
    widened = widened.reshape(row_total, adapter_total, 2, rank_width)
    values = jnp.einsum("racq,acqh->rch", widened, up_table, preferred_element_type=jnp.float32)
    return values.astype(jnp.bfloat16)


def on_device(
    hidden,
    gain,
    key_value_weight,
    adapter_down_weight,
    adapter_up_weight,
    language_pair_index,
    adapter_row_index,
):
    tok_count = hidden.shape[0]
    model_width = hidden.shape[1]
    owner_count = lax.axis_size("ad")
    by_holder = adapter_down_weight.shape[0]
    column_portion = adapter_down_weight.shape[1]
    head_cols = key_value_weight.shape[2]
    row_quota = tok_count // owner_count
    wide_hidden = hidden.astype(jnp.float32)
    inv_rms = lax.rsqrt(jnp.mean(wide_hidden * wide_hidden, axis=-1, keepdims=True) + epsilon)
    normed = (wide_hidden * inv_rms * gain.astype(jnp.float32)).astype(jnp.bfloat16)
    base_projection = jnp.dot(
        normed,
        key_value_weight.reshape(model_width, 2 * head_cols),
        preferred_element_type=jnp.float32,
    ).reshape(tok_count, 2, head_cols)
    own_cols = lax.dynamic_slice_in_dim(
        normed, lax.axis_index("tp") * column_portion, column_portion, 1
    )
    slot_ids = adapter_row_index[language_pair_index]
    owner_ids = slot_ids // by_holder
    local_ids = slot_ids % by_holder
    owner_labels = jnp.arange(owner_count, dtype=jnp.int32)
    capacity = 4 * row_quota
    onehot = (owner_ids[:, None] == owner_labels[None, :]).astype(jnp.int32)
    before = jnp.cumsum(onehot, axis=0) - onehot
    bucket_pos = jnp.sum(before * onehot, axis=1)
    total_slots = owner_count * capacity
    dest_slot = jnp.where(owner_ids < owner_count, owner_ids * capacity + bucket_pos, total_slots)
    slot_labels = jnp.arange(total_slots, dtype=jnp.int32)
    selector = slot_labels[:, None] == dest_slot[None, :]
    selector_bf = selector.astype(jnp.bfloat16)
    send_rows = jnp.dot(selector_bf, own_cols, preferred_element_type=jnp.float32).astype(
        jnp.bfloat16
    )
    send_rows = send_rows.reshape(owner_count, capacity, column_portion)
    filled = jnp.any(selector, axis=1)
    picked_ids = jnp.sum(jnp.where(selector, local_ids[None, :], 0), axis=1)
    send_ids = jnp.where(filled, picked_ids, by_holder).reshape(owner_count, capacity)
    received_rows = lax.all_to_all(send_rows, "ad", split_axis=0, concat_axis=0, tiled=True)
    got_ids = lax.all_to_all(send_ids, "ad", split_axis=0, concat_axis=0, tiled=True)
    source_count = got_ids.shape[0]
    element_count = got_ids.shape[1]
    flat_ids = got_ids.reshape(source_count * element_count)
    partial_low, row_mask = down_local(
        received_rows.reshape(source_count * element_count, column_portion),
        flat_ids,
        adapter_down_weight,
    )
    summed_output = lax.psum(partial_low, "tp")
    delta_rows = upward_delta(summed_output, row_mask, adapter_up_weight).reshape(
        source_count, element_count, 2, head_cols
    )
    returned = lax.all_to_all(delta_rows, "ad", split_axis=0, concat_axis=0, tiled=True)
    flat_back = returned.reshape(total_slots, 2 * head_cols)
    back_rows = jnp.einsum("st,sc->tc", selector_bf, flat_back, preferred_element_type=jnp.float32)
    delta_by_row = back_rows.astype(jnp.bfloat16).reshape(tok_count, 2, head_cols)
    return (base_projection + adapter_scale * delta_by_row.astype(jnp.float32)).astype(jnp.bfloat16)


def solution(mesh):
    return jax.shard_map(
        on_device,
        mesh=mesh,
        in_specs=(
            P("ad", None),
            P(),
            P(None, None, "tp"),
            P("ad", "tp", None),
            P("ad", None, None, "tp"),
            P("ad"),
            P(),
        ),
        out_specs=P("ad", None, "tp"),
        check_vma=False,
    )
```

profile of v0, /device:TPU:6, one launch (start us, length us, event | category | flops | bytes accessed | tf_op | source)
XLA Modules:
  0.0 251.6 jit_solution(11058479754245148850)
XLA Ops:
  0.0 0.0 copy-start
  0.0 2.1 fusion.34
  2.1 2.1 fusion.35
  4.1 2.1 fusion.36
  6.2 1.6 fusion.37
  7.8 40.5 %add_select_fusion = (s32[448]{0:T(512)S(1)}, s32[448]{0:T(512)S(1)}) fusion(s32[]{:T(128)} %bitcast.66, s32[]{:T(128)} %bitcast.65, s32[]{:T(128)} %bitcast.64, s32[]{:T(128)} %bitcast.63, s32[]{:T(128)} %bitcast.62, s32[]{:T(128)} %bitcast.61, s32[]{:T(128)} %bitcast.60, s32[]{:T(128)} %bitcast.59, s32[]{:T(128)} %bitcast.58, s32[]{:T(128)} %bitcast.57, ...), kind=kLoop, calls=%fused_computation.46 | loop fusion | flops 62720 | bytes 5632 | tf_op jit(solution)/shard_map/jit(remainder)/select_n | solution.py:59
  48.4 1.2 reduce-window.6
  49.6 0.2 slice_reduce_fusion
  49.8 0.1 bitcast_bitcast_fusion.1
  50.0 0.6 fusion.6
  50.5 0.4 select_reduce_fusion
  51.0 0.7 select_n.72
  51.7 11.5 %all-to-all-start = ((s32[32,1,56]{2,1,0:T(1,128)}), s32[32,1,56]{2,1,0:T(1,128)S(1)}, u32[]{:S(2)}, u32[]{:S(2)}) async-start(s32[32,1,56]{2,1,0:T(1,128)} %select_n.72), calls=%async_computation | async-start | bytes 32768 | tf_op jit(solution)/shard_map/all_to_all | solution.py:78
  63.2 0.7 convert_element_type.37
  63.9 4.6 %fusion = f32[448]{0:T(512)S(1)} fusion(bf16[448,8192]{1,0:T(8,128)(2,1)} %param.7), kind=kLoop, calls=%fused_computation.2 | loop fusion | flops 11009600 | bytes 7341824 | tf_op jit(solution)/shard_map/reduce_sum | solution.py:47
  68.5 5.5 %fusion.2 = bf16[448,8192]{1,0:T(8,128)(2,1)S(1)} fusion(bf16[448,8192]{1,0:T(8,128)(2,1)} %param.7, f32[8192]{0:T(1024)S(1)} %convert_element_type.37, f32[448]{0:T(512)S(1)} %add_rsqrt_fusion), kind=kLoop, calls=%fused_computation.4 | loop fusion | flops 14680064 | bytes 14714624 | tf_op jit(solution)/shard_map/convert_element_type | solution.py:48
  74.1 0.0 copy-start.1
  74.1 3.0 %copy-done.1 = bf16[448,8192]{1,0:T(8,128)(2,1)} copy-done((bf16[448,8192]{1,0:T(8,128)(2,1)}, bf16[448,8192]{1,0:T(8,128)(2,1)S(1)}, u32[]{:S(2)}) %copy-start.1) | copy-done | bytes 7340056
  77.0 4.1 %convolution_convert_fusion = bf16[1792,1024]{1,0:T(8,128)(2,1)} fusion(s32[448]{0:T(512)S(1)} %add_select_fusion.2, bf16[448,8192]{1,0:T(8,128)(2,1)S(1)} %fusion.2, s32[]{:T(128)S(6)} %select_n.73), kind=kOutput, calls=%fused_computation.8 | convolution fusion | flops 1646804992 | bytes 4589572 | tf_op jit(solution)/shard_map/dot_general | solution.py:70
  81.2 0.0 all-to-all-done
  81.2 9.9 %all-to-all-start.1 = ((bf16[32,56,1024]{2,1,0:T(8,128)(2,1)}), bf16[32,56,1024]{2,1,0:T(8,128)(2,1)}, u32[]{:S(2)}, u32[]{:S(2)}) async-start(bf16[32,56,1024]{2,1,0:T(8,128)(2,1)} %bitcast.119), calls=%async_computation.1 | async-start | bytes 7340032 | tf_op jit(solution)/shard_map/all_to_all | solution.py:77
  91.1 0.5 broadcast.414
  91.6 0.7 reduce.5
  92.3 0.1 eq.63
  92.4 84.1 %all-to-all-done.1 = bf16[32,56,1024]{2,1,0:T(8,128)(2,1)} async-done(((bf16[32,56,1024]{2,1,0:T(8,128)(2,1)}), bf16[32,56,1024]{2,1,0:T(8,128)(2,1)}, u32[]{:S(2)}, u32[]{:S(2)}) %all-to-all-start.1) | async-done | bytes 3670048 | tf_op jit(solution)/shard_map/all_to_all | solution.py:77
  176.5 0.0 copy-done
  176.5 0.0 copy-start.2
  176.5 3.2 %fusion.10 = f32[1792,128]{1,0:T(8,128)S(1)} fusion(bf16[1792,1024,1]{1,0,2:T(8,128)(2,1)} %bitcast.70, bf16[2,1024,128]{2,1,0:T(8,128)(2,1)S(1)} %copy-done, pred[1792,2]{0,1:T(4,128)(4,1)S(1)} %iota_compare_fusion.13), kind=kOutput, calls=%fused_computation.18 | convolution fusion | flops 940212224 | bytes 5115392 | tf_op jit(solution)/shard_map/rc,acm->ram/dot_general | solution.py:14
  179.7 28.7 %all-reduce.2 = bf16[1792,128]{1,0:T(8,128)(2,1)S(1)} all-reduce(f32[1792,128]{1,0:T(8,128)S(1)} %fusion.10), channel_id=1, replica_groups=mesh['tp'=8,'ad'=32] {'tp'}, use_global_device_ids=true, to_apply=%region_7.8 | all-reduce | flops 229376 | bytes 1376256 | tf_op jit(solution)/shard_map/psum | solution.py:87
  208.4 0.2 copy.37
  208.6 0.0 copy-done.2
  208.6 0.5 fusion.7
  209.1 1.9 copy.39
  211.0 6.2 %all-to-all-start.2 = ((bf16[32,56,2,128]{3,2,1,0:T(2,128)(2,1)}), bf16[32,56,2,128]{3,2,1,0:T(2,128)(2,1)S(1)}, u32[]{:S(2)}, u32[]{:S(2)}) async-start(bf16[32,56,2,128]{3,2,1,0:T(2,128)(2,1)} %copy.39), calls=%async_computation.2 | async-start | bytes 1835008 | tf_op jit(solution)/shard_map/all_to_all | solution.py:91
  217.2 4.8 %copy.58 = bf16[1024,8,2,128]{3,1,2,0:T(8,128)(2,1)} copy(bf16[1024,8,2,128]{3,2,1,0:T(2,128)(2,1)} %bitcast.117) | data formatting | bytes 8388608
  222.0 6.4 %copy.34 = bf16[256,8192]{1,0:T(8,128)(2,1)} copy(bf16[256,8192]{0,1:T(8,128)(2,1)} %bitcast.116) | data formatting | bytes 8388608 | tf_op jit(solution)/shard_map/dot_general | solution.py:49
  228.4 15.2 %all-to-all-done.2 = bf16[32,56,2,128]{3,2,1,0:T(2,128)(2,1)S(1)} async-done(((bf16[32,56,2,128]{3,2,1,0:T(2,128)(2,1)}), bf16[32,56,2,128]{3,2,1,0:T(2,128)(2,1)S(1)}, u32[]{:S(2)}, u32[]{:S(2)}) %all-to-all-start.2) | async-done | bytes 917536 | tf_op jit(solution)/shard_map/all_to_all | solution.py:91
  243.5 0.7 fusion.17
  244.3 6.4 %fusion.18 = bf16[448,2,128]{2,0,1:T(8,128)(2,1)S(1)} fusion(bf16[2,128,8192]{2,1,0:T(8,128)(2,1)} %bitcast.118, bf16[448,8192]{1,0:T(8,128)(2,1)} %copy-done.1, f32[56,2,8,128]{3,2,1,0:T(8,128)S(1)} %fusion.17), kind=kOutput, calls=%fused_computation.24 | convolution fusion | flops 1879277568 | bytes 12222464 | tf_op jit(solution)/shard_map/dot_general | solution.py:49
  250.7 0.9 copy.41
  (10 shorter events, 0.1 us)
Async XLA Ops:
  0.0 176.5 %copy-start = (bf16[2,1024,128]{2,1,0:T(8,128)(2,1)S(1)}, bf16[2,1024,128]{2,1,0:T(8,128)(2,1)}, u32[]{:S(2)}) copy-start(bf16[2,1024,128]{2,1,0:T(8,128)(2,1)} %param.10) | copy-start | bytes 1572868
  51.7 29.5 %all-to-all-start = ((s32[32,1,56]{2,1,0:T(1,128)}), s32[32,1,56]{2,1,0:T(1,128)S(1)}, u32[]{:S(2)}, u32[]{:S(2)}) async-start(s32[32,1,56]{2,1,0:T(1,128)} %select_n.72), calls=%async_computation | async-start | bytes 32768 | tf_op jit(solution)/shard_map/all_to_all | solution.py:78
  74.1 3.0 %copy-start.1 = (bf16[448,8192]{1,0:T(8,128)(2,1)}, bf16[448,8192]{1,0:T(8,128)(2,1)S(1)}, u32[]{:S(2)}) copy-start(bf16[448,8192]{1,0:T(8,128)(2,1)S(1)} %fusion.2) | copy-start | bytes 22020100
  81.2 95.3 %all-to-all-start.1 = ((bf16[32,56,1024]{2,1,0:T(8,128)(2,1)}), bf16[32,56,1024]{2,1,0:T(8,128)(2,1)}, u32[]{:S(2)}, u32[]{:S(2)}) async-start(bf16[32,56,1024]{2,1,0:T(8,128)(2,1)} %bitcast.119), calls=%async_computation.1 | async-start | bytes 7340032 | tf_op jit(solution)/shard_map/all_to_all | solution.py:77
  176.5 32.1 %copy-start.2 = (bf16[2,2,64,128]{3,2,1,0:T(8,128)(2,1)S(1)}, bf16[2,2,64,128]{3,2,1,0:T(8,128)(2,1)}, u32[]{:S(2)}) copy-start(bf16[2,2,64,128]{3,2,1,0:T(8,128)(2,1)} %param.11) | copy-start | bytes 196612
  211.0 32.6 %all-to-all-start.2 = ((bf16[32,56,2,128]{3,2,1,0:T(2,128)(2,1)}), bf16[32,56,2,128]{3,2,1,0:T(2,128)(2,1)S(1)}, u32[]{:S(2)}, u32[]{:S(2)}) async-start(bf16[32,56,2,128]{3,2,1,0:T(2,128)(2,1)} %copy.39), calls=%async_computation.2 | async-start | bytes 1835008 | tf_op jit(solution)/shard_map/all_to_all | solution.py:91
where the time goes:
time: 253 us; the launch traced here: 252 us
  waiting for transfers between devices  99.2 us (39%)
  other arithmetic  54.5 us (22%)
  blocking collectives  28.7 us (11%)
  starting transfers between devices  27.6 us (11%)
  local copies, waits for them, and re-layouts  26.5 us (10%)
  matrix products  14.9 us (6%)
    all_to_all x1, waiting for transfers between devices, on_device(): lax.all_to_all(send_rows, 'ad', split_axis=0, concat_axis=0, tiled=True)  84.1 us
    select_n x1, other arithmetic, on_device(): local_ids = slot_ids % by_holder  40.5 us
    psum x1, blocking collectives, on_device(): summed_output = lax.psum(partial_low, 'tp')  28.7 us
    all_to_all x1, waiting for transfers between devices, on_device(): lax.all_to_all(delta_rows, 'ad', split_axis=0, concat_axis=0, tiled=True)  15.2 us
    all_to_all x1, starting transfers between devices, on_device(): lax.all_to_all(send_ids, 'ad', split_axis=0, concat_axis=0, tiled=True)  11.5 us
    all_to_all x1, starting transfers between devices, on_device(): lax.all_to_all(send_rows, 'ad', split_axis=0, concat_axis=0, tiled=True)  9.9 us
    gather x4, local copies, waits for them, and re-layouts, on_device(): slot_ids = adapter_row_index[language_pair_index]  7.79 us
    unnamed x7, local copies, waits for them, and re-layouts  7.74 us
  transfers between devices with their start and end apart: 3, of which 2 were waited for; matrix products, arithmetic and copies ran while one was open for 11% of the time, Pallas kernels for 0%

commit v1 on v0

--- a/solution.py
+++ b/solution.py
@@ -5,6 +5,10 @@
 
 epsilon = 1e-05
 adapter_scale = 0.5
+
+
+def _shape_indices(x_local):
+    return jnp.sum(jax.lax.all_gather(x_local, "tp"), 0)
 
 
 def down_local(rows_in, row_ids, down_table):
@@ -84,7 +88,7 @@
         flat_ids,
         adapter_down_weight,
     )
-    summed_output = lax.psum(partial_low, "tp")
+    summed_output = _shape_indices(partial_low)
     delta_rows = upward_delta(summed_output, row_mask, adapter_up_weight).reshape(
         source_count, element_count, 2, head_cols
     )

time: 253 us -> 291 us (1.15)
  waiting for transfers between devices: 99.2 us -> 143 us
  blocking collectives: 28.7 us -> 0 us
  between operations: 0.2 us -> 13.6 us
  starting transfers between devices: 27.6 us -> 31.5 us
  other arithmetic: 54.5 us -> 58 us
    all_gather x0 -> x1, waiting for transfers between devices: none -> 43.7 us  [_shape_indices(): return jnp.sum(jax.lax.all_gather(x_local, 'tp'), 0)]
    psum x1 -> x0, blocking collectives: 28.7 us -> none  [on_device(): summed_output = lax.psum(partial_low, 'tp')]
    all_to_all x1, starting transfers between devices: 6.24 us -> 9.94 us  [on_device(): lax.all_to_all(delta_rows, 'ad', split_axis=0, concat_axis=0, tiled=True)]
    reduce_sum x0 -> x1, other arithmetic: none -> 3.51 us  [_shape_indices(): return jnp.sum(jax.lax.all_gather(x_local, 'tp'), 0)]
  transfers between devices with their start and end apart: 3 -> 4, of which waited for: 2 -> 3; matrix products, arithmetic and copies ran while one was open for 11% -> 10% of each run, Pallas kernels for 0% -> 0%
where the time goes in v1:
time: 291 us; the launch traced here: 288 us
  waiting for transfers between devices  143 us (49%)
  other arithmetic  58 us (20%)
  starting transfers between devices  31.5 us (11%)
  local copies, waits for them, and re-layouts  26.5 us (9%)
  matrix products  15.9 us (5%)
  between operations  13.6 us (5%)
    all_to_all x1, waiting for transfers between devices, on_device(): lax.all_to_all(send_rows, 'ad', split_axis=0, concat_axis=0, tiled=True)  83.8 us
    all_gather x1, waiting for transfers between devices, _shape_indices(): return jnp.sum(jax.lax.all_gather(x_local, 'tp'), 0)  43.7 us
    select_n x1, other arithmetic, on_device(): local_ids = slot_ids % by_holder  40.5 us
    all_to_all x1, waiting for transfers between devices, on_device(): lax.all_to_all(delta_rows, 'ad', split_axis=0, concat_axis=0, tiled=True)  15.1 us
    all_to_all x1, starting transfers between devices, on_device(): lax.all_to_all(send_ids, 'ad', split_axis=0, concat_axis=0, tiled=True)  11.5 us
    all_to_all x1, starting transfers between devices, on_device(): lax.all_to_all(delta_rows, 'ad', split_axis=0, concat_axis=0, tiled=True)  9.94 us
    all_to_all x1, starting transfers between devices, on_device(): lax.all_to_all(send_rows, 'ad', split_axis=0, concat_axis=0, tiled=True)  9.9 us
    gather x4, local copies, waits for them, and re-layouts, on_device(): slot_ids = adapter_row_index[language_pair_index]  7.79 us
  transfers between devices with their start and end apart: 4, of which 3 were waited for; matrix products, arithmetic and copies ran while one was open for 10% of the time, Pallas kernels for 0%

profile of v1, /device:TPU:6, one launch (start us, length us, event | category | flops | bytes accessed | tf_op | source)
XLA Modules:
  0.0 288.1 jit_solution(17785102270740880417)
XLA Ops:
  6.5 0.0 copy-start
  6.5 2.1 fusion.34
  8.6 2.1 fusion.35
  10.7 2.1 fusion.36
  12.8 1.6 fusion.37
  14.3 40.5 %add_select_fusion = (s32[448]{0:T(512)S(1)}, s32[448]{0:T(512)S(1)}) fusion(s32[]{:T(128)} %bitcast.66, s32[]{:T(128)} %bitcast.65, s32[]{:T(128)} %bitcast.64, s32[]{:T(128)} %bitcast.63, s32[]{:T(128)} %bitcast.62, s32[]{:T(128)} %bitcast.61, s32[]{:T(128)} %bitcast.60, s32[]{:T(128)} %bitcast.59, s32[]{:T(128)} %bitcast.58, s32[]{:T(128)} %bitcast.57, ...), kind=kLoop, calls=%fused_computation.46 | loop fusion | flops 62720 | bytes 5632 | tf_op jit(solution)/shard_map/jit(remainder)/select_n | solution.py:63
  54.9 1.2 reduce-window.6
  56.1 0.2 slice_reduce_fusion
  56.4 0.1 bitcast_bitcast_fusion.1
  56.5 0.6 fusion.6
  57.1 0.4 select_reduce_fusion
  57.5 0.7 select_n.72
  58.2 11.5 %all-to-all-start = ((s32[32,1,56]{2,1,0:T(1,128)}), s32[32,1,56]{2,1,0:T(1,128)S(1)}, u32[]{:S(2)}, u32[]{:S(2)}) async-start(s32[32,1,56]{2,1,0:T(1,128)} %select_n.72), calls=%async_computation | async-start | bytes 32768 | tf_op jit(solution)/shard_map/all_to_all | solution.py:82
  69.7 0.7 convert_element_type.44
  70.4 4.6 %fusion = f32[448]{0:T(512)S(1)} fusion(bf16[448,8192]{1,0:T(8,128)(2,1)} %param.7), kind=kLoop, calls=%fused_computation.2 | loop fusion | flops 11009600 | bytes 7341824 | tf_op jit(solution)/shard_map/reduce_sum | solution.py:51
  75.1 5.5 %fusion.2 = bf16[448,8192]{1,0:T(8,128)(2,1)S(1)} fusion(bf16[448,8192]{1,0:T(8,128)(2,1)} %param.7, f32[8192]{0:T(1024)S(1)} %convert_element_type.44, f32[448]{0:T(512)S(1)} %add_rsqrt_fusion), kind=kLoop, calls=%fused_computation.4 | loop fusion | flops 14680064 | bytes 14714624 | tf_op jit(solution)/shard_map/convert_element_type | solution.py:52
  80.6 0.0 copy-start.1
  80.6 3.0 %copy-done.1 = bf16[448,8192]{1,0:T(8,128)(2,1)} copy-done((bf16[448,8192]{1,0:T(8,128)(2,1)}, bf16[448,8192]{1,0:T(8,128)(2,1)S(1)}, u32[]{:S(2)}) %copy-start.1) | copy-done | bytes 7340056
  83.6 4.1 %convolution_convert_fusion = bf16[1792,1024]{1,0:T(8,128)(2,1)} fusion(s32[448]{0:T(512)S(1)} %add_select_fusion.2, bf16[448,8192]{1,0:T(8,128)(2,1)S(1)} %fusion.2, s32[]{:T(128)S(6)} %select_n.73), kind=kOutput, calls=%fused_computation.8 | convolution fusion | flops 1646804992 | bytes 4589572 | tf_op jit(solution)/shard_map/dot_general | solution.py:74
  87.7 0.0 all-to-all-done
  87.7 9.9 %all-to-all-start.1 = ((bf16[32,56,1024]{2,1,0:T(8,128)(2,1)}), bf16[32,56,1024]{2,1,0:T(8,128)(2,1)}, u32[]{:S(2)}, u32[]{:S(2)}) async-start(bf16[32,56,1024]{2,1,0:T(8,128)(2,1)} %bitcast.121), calls=%async_computation.1 | async-start | bytes 7340032 | tf_op jit(solution)/shard_map/all_to_all | solution.py:81
  97.6 0.2 all-gather.3.cloned.1.call-start
  97.8 0.5 broadcast.414
  98.3 0.7 reduce.5
  99.0 0.1 eq.63
  99.2 83.8 %all-to-all-done.1 = bf16[32,56,1024]{2,1,0:T(8,128)(2,1)} async-done(((bf16[32,56,1024]{2,1,0:T(8,128)(2,1)}), bf16[32,56,1024]{2,1,0:T(8,128)(2,1)}, u32[]{:S(2)}, u32[]{:S(2)}) %all-to-all-start.1) | async-done | bytes 3670048 | tf_op jit(solution)/shard_map/all_to_all | solution.py:81
  183.0 0.0 copy-done
  183.0 4.2 %fusion.10 = f32[1792,128]{1,0:T(8,128)} fusion(bf16[1792,1024,1]{1,0,2:T(8,128)(2,1)} %bitcast.70, bf16[2,1024,128]{2,1,0:T(8,128)(2,1)S(1)} %copy-done, pred[1792,2]{0,1:T(4,128)(4,1)S(1)} %iota_compare_fusion.13), kind=kOutput, calls=%fused_computation.18 | convolution fusion | flops 940212224 | bytes 5115392 | tf_op jit(solution)/shard_map/rc,acm->ram/dot_general | solution.py:18
  187.1 0.0 all-gather.3.cloned.1.call-update
  187.2 43.7 %all-gather.3.cloned.1.call-done = f32[14336,128]{1,0:T(8,128)} async-done(((f32[1792,128]{1,0:T(8,128)}), f32[14336,128]{1,0:T(8,128)}) %all-gather.3.cloned.1.call-update) | async-done | bytes 7340048 | tf_op jit(solution)/shard_map/all_gather | solution.py:11
  230.8 0.0 copy-start.2
  230.8 3.5 %reduce_sum.49 = bf16[1792,128]{1,0:T(8,128)(2,1)S(1)} reduce(f32[8,1792,128]{2,1,0:T(8,128)} %bitcast.118, f32[]{:T(128)} %constant.46.clone.1), dimensions={0}, to_apply=%region_7.8 | reduce | flops 1605632 | bytes 7798788 | tf_op jit(solution)/shard_map/reduce_sum | solution.py:11
  234.4 0.2 copy.29
  234.6 0.0 copy-done.2
  234.6 0.5 fusion.7
  235.1 1.9 copy.31
  237.0 9.9 %all-to-all-start.2 = ((bf16[32,56,2,128]{3,2,1,0:T(2,128)(2,1)}), bf16[32,56,2,128]{3,2,1,0:T(2,128)(2,1)S(1)}, u32[]{:S(2)}, u32[]{:S(2)}) async-start(bf16[32,56,2,128]{3,2,1,0:T(2,128)(2,1)} %copy.31), calls=%async_computation.2 | async-start | bytes 1835008 | tf_op jit(solution)/shard_map/all_to_all | solution.py:95
  246.9 4.8 %copy.50 = bf16[1024,8,2,128]{3,1,2,0:T(8,128)(2,1)} copy(bf16[1024,8,2,128]{3,2,1,0:T(2,128)(2,1)} %bitcast.119) | data formatting | bytes 8388608
  251.7 6.4 %copy.26 = bf16[256,8192]{1,0:T(8,128)(2,1)} copy(bf16[256,8192]{0,1:T(8,128)(2,1)} %bitcast.117) | data formatting | bytes 8388608 | tf_op jit(solution)/shard_map/dot_general | solution.py:53
  258.1 15.1 %all-to-all-done.2 = bf16[32,56,2,128]{3,2,1,0:T(2,128)(2,1)S(1)} async-done(((bf16[32,56,2,128]{3,2,1,0:T(2,128)(2,1)}), bf16[32,56,2,128]{3,2,1,0:T(2,128)(2,1)S(1)}, u32[]{:S(2)}, u32[]{:S(2)}) %all-to-all-start.2) | async-done | bytes 917536 | tf_op jit(solution)/shard_map/all_to_all | solution.py:95
  273.2 0.7 fusion.17
  274.0 6.4 %fusion.18 = bf16[448,2,128]{2,0,1:T(8,128)(2,1)S(1)} fusion(bf16[2,128,8192]{2,1,0:T(8,128)(2,1)} %bitcast.120, bf16[448,8192]{1,0:T(8,128)(2,1)} %copy-done.1, f32[56,2,8,128]{3,2,1,0:T(8,128)S(1)} %fusion.17), kind=kOutput, calls=%fused_computation.24 | convolution fusion | flops 1879277568 | bytes 12222464 | tf_op jit(solution)/shard_map/dot_general | solution.py:53
  280.3 0.9 copy.33
  (10 shorter events, 0.1 us)
Async XLA Ops:
  6.5 176.5 %copy-start = (bf16[2,1024,128]{2,1,0:T(8,128)(2,1)S(1)}, bf16[2,1024,128]{2,1,0:T(8,128)(2,1)}, u32[]{:S(2)}) copy-start(bf16[2,1024,128]{2,1,0:T(8,128)(2,1)} %param.10) | copy-start | bytes 1572868
  58.2 29.5 %all-to-all-start = ((s32[32,1,56]{2,1,0:T(1,128)}), s32[32,1,56]{2,1,0:T(1,128)S(1)}, u32[]{:S(2)}, u32[]{:S(2)}) async-start(s32[32,1,56]{2,1,0:T(1,128)} %select_n.72), calls=%async_computation | async-start | bytes 32768 | tf_op jit(solution)/shard_map/all_to_all | solution.py:82
  80.6 3.0 %copy-start.1 = (bf16[448,8192]{1,0:T(8,128)(2,1)}, bf16[448,8192]{1,0:T(8,128)(2,1)S(1)}, u32[]{:S(2)}) copy-start(bf16[448,8192]{1,0:T(8,128)(2,1)S(1)} %fusion.2) | copy-start | bytes 22020100
  87.7 95.3 %all-to-all-start.1 = ((bf16[32,56,1024]{2,1,0:T(8,128)(2,1)}), bf16[32,56,1024]{2,1,0:T(8,128)(2,1)}, u32[]{:S(2)}, u32[]{:S(2)}) async-start(bf16[32,56,1024]{2,1,0:T(8,128)(2,1)} %bitcast.121), calls=%async_computation.1 | async-start | bytes 7340032 | tf_op jit(solution)/shard_map/all_to_all | solution.py:81
  97.6 133.2 %all-gather.3.cloned.1.call-start = ((), (), s32[]{:S(2)}) async-start(), calls=%async_computation.3 | async-start | bytes 8257536 | tf_op jit(solution)/shard_map/all_gather | solution.py:11
  230.8 3.7 %copy-start.2 = (bf16[2,2,64,128]{3,2,1,0:T(8,128)(2,1)S(1)}, bf16[2,2,64,128]{3,2,1,0:T(8,128)(2,1)}, u32[]{:S(2)}) copy-start(bf16[2,2,64,128]{3,2,1,0:T(8,128)(2,1)} %param.11) | copy-start | bytes 196612
  237.0 36.2 %all-to-all-start.2 = ((bf16[32,56,2,128]{3,2,1,0:T(2,128)(2,1)}), bf16[32,56,2,128]{3,2,1,0:T(2,128)(2,1)S(1)}, u32[]{:S(2)}, u32[]{:S(2)}) async-start(bf16[32,56,2,128]{3,2,1,0:T(2,128)(2,1)} %copy.31), calls=%async_computation.2 | async-start | bytes 1835008 | tf_op jit(solution)/shard_map/all_to_all | solution.py:95
Sparse Core Ops, SparseCore 0:
  187.3 43.5 all-gather.2
